TPU v7x, 256 devices: a whole 4x4x8 slice. The times are simulated.
256 devices in a mesh: grp: 16 (over x, y), seq: 16 (over z, core).
Axes of the slice: x: 4, y: 4, z: 8, core: 2. Of those that a mesh axis runs over, the one named last changes fastest.
Arguments:
- events: bfloat16 [65536, 1024], P(('grp', 'seq')), may hold values from -6 to 6
- lengths: int32 [256, 16], P(('grp', 'seq')), may hold values from 1 to 24, as said below
- destinations: int32 [256, 16], P(('grp', 'seq')), may hold values from 0 to 15, as said below
- history: int32 [65536], P(('grp', 'seq')), may hold values from 0 to 8191, as said below
- negatives: int32 [65536, 3], P(('grp', 'seq')), may hold values from 0 to 8191, as said below
- in_weight: bfloat16 [1024, 2048], replicated, may hold values from -0.1875 to 0.1875
- out_weight: bfloat16 [1024, 512], replicated, may hold values from -0.25 to 0.25
- item_table: bfloat16 [8192, 1024], P('seq'), may hold values from -0.1875 to 0.1875
Outputs:
- layer_out: bfloat16 [65536, 1024], P(('grp', 'seq'))
- in_grad: float32 [1024, 2048], P('seq')
- out_grad: float32 [1024, 512], P('seq')
- table_grad: float32 [8192, 1024], P('seq')
Inputs may be any that keep to these rules, and one draw needn't show every extreme that they name: Each loader device holds 16 users whose lengths sum to 256; the longest history is 24. `destinations`: the 16 users of a loader device go to the 16 different devices of its group, one to each, and every device of a group receives users with 256 rows in all. `history`: item i lies in row i % 512 of owner i // 512. The 4 candidates of an event lie on 4 different owners, and after the relayout every device holds exactly 64 candidates of each owner. `negatives`: numbered as history; see there.
All inputs are finite; a program needn't handle non-finite values.
Results may differ from a plain program's by a relative error of at most 0.02.
Values may be sent and summed in bfloat16 or wider, within the bound.
A program may use at most 128 MiB of HBM per device.

v0:
```python
import jax
import jax.numpy as jnp
from jax import lax
from jax.sharding import PartitionSpec as P

D = 1024
HEADS = 4
HEAD_DIM = 128
NCAND = 4
VOCAB_DEV = 512
epsilon = 1e-05
softmax_warmth = 0.05


def center_scale(values):
    average = jnp.mean(values, -1, keepdims=True)
    centered = values - average
    inverse = lax.rsqrt(jnp.mean(centered * centered, -1, keepdims=True) + epsilon)
    return (centered * inverse, inverse)


def silu_slope(values):
    sigmoid = jax.nn.sigmoid(values)
    return sigmoid * (1.0 + values * (1.0 - sigmoid))


def batch_stacked(pattern, first_operand, second_operand):
    return jnp.einsum(pattern, first_operand, second_operand, preferred_element_type=jnp.float32)


def layer_forward(tokens, attend_mask, in_weight, out_weight, batch_count):
    hidden_width = out_weight.shape[1]
    scoring_scale = HEAD_DIM ** (-0.5)
    features = tokens.astype(jnp.float32)
    normed_in = center_scale(features)[0].astype(jnp.bfloat16)
    preact = jnp.dot(normed_in, in_weight, preferred_element_type=jnp.float32)
    projected = jax.nn.silu(preact).astype(jnp.bfloat16)
    gate_part = projected[:, :hidden_width]
    value_portion = projected[:, hidden_width : 2 * hidden_width].reshape(
        batch_count, -1, hidden_width
    )
    query_portion = projected[:, 2 * hidden_width : 3 * hidden_width].reshape(
        batch_count, -1, hidden_width
    )
    key_portion = projected[:, 3 * hidden_width :].reshape(batch_count, -1, hidden_width)
    score_list, weight_pieces, output_pieces = ([], [], [])
    for current_head in range(HEADS):
        column_begin = current_head * HEAD_DIM
        column_end = column_begin + HEAD_DIM
        attention_scores = (
            batch_stacked(
                "ptx,pux->ptu",
                query_portion[..., column_begin:column_end],
                key_portion[..., column_begin:column_end],
            )
            * scoring_scale
        )
        attention_weight = (jax.nn.silu(attention_scores) * attend_mask).astype(jnp.bfloat16)
        output_pieces.append(
            batch_stacked(
                "fjz,fzy->fjy", attention_weight, value_portion[..., column_begin:column_end]
            )
        )
        score_list.append(attention_scores)
        weight_pieces.append(attention_weight)
    attended = jnp.concatenate(output_pieces, -1).reshape(-1, hidden_width)
    normed, inverse = center_scale(attended)
    gated_rows = (normed * gate_part.astype(jnp.float32)).astype(jnp.bfloat16)
    result = features + lax.dot_general(
        gated_rows, out_weight, (((1,), (1,)), ((), ())), preferred_element_type=jnp.float32
    )
    saved_state = (
        normed_in,
        preact,
        gate_part,
        value_portion,
        query_portion,
        key_portion,
        score_list,
        weight_pieces,
        normed,
        inverse,
        gated_rows,
    )
    return (result, saved_state)


def layer_backward(upstream, saved_state, attend_mask, out_weight, batch_count):
    (
        normed_in,
        preact,
        gate_part,
        value_portion,
        query_portion,
        key_portion,
        score_list,
        weight_pieces,
        normed,
        inverse,
        gated_rows,
    ) = saved_state
    hidden_width = out_weight.shape[1]
    scoring_scale = HEAD_DIM ** (-0.5)
    upstream_b = upstream.astype(jnp.bfloat16)
    grad_gated = jnp.dot(upstream_b, out_weight, preferred_element_type=jnp.float32)
    grad_gate = grad_gated * normed
    grad_normed = grad_gated * gate_part.astype(jnp.float32)
    grad_attended = inverse * (
        grad_normed
        - jnp.mean(grad_normed, -1, keepdims=True)
        - normed * jnp.mean(grad_normed * normed, -1, keepdims=True)
    )
    grad_attended = grad_attended.astype(jnp.bfloat16).reshape(batch_count, -1, hidden_width)
    value_gradient, query_gradient, key_gradient = ([], [], [])
    for current_head in range(HEADS):
        column_begin = current_head * HEAD_DIM
        column_end = column_begin + HEAD_DIM
        gradient_portion = grad_attended[..., column_begin:column_end]
        weight_gradient = batch_stacked(
            "ptx,pux->ptu", gradient_portion, value_portion[..., column_begin:column_end]
        )
        value_gradient.append(
            batch_stacked("hyo,hyx->hox", weight_pieces[current_head], gradient_portion)
        )
        score_gradient = (
            weight_gradient * attend_mask * silu_slope(score_list[current_head]) * scoring_scale
        ).astype(jnp.bfloat16)
        query_gradient.append(
            batch_stacked("fjz,fzy->fjy", score_gradient, key_portion[..., column_begin:column_end])
        )
        key_gradient.append(
            batch_stacked(
                "hyo,hyx->hox", score_gradient, query_portion[..., column_begin:column_end]
            )
        )
    grad_project = jnp.concatenate(
        [
            grad_gate,
            jnp.concatenate(value_gradient, -1).reshape(-1, hidden_width),
            jnp.concatenate(query_gradient, -1).reshape(-1, hidden_width),
            jnp.concatenate(key_gradient, -1).reshape(-1, hidden_width),
        ],
        -1,
    )
    grad_preact = (grad_project * silu_slope(preact)).astype(jnp.bfloat16)
    return (normed_in, grad_preact, upstream_b, gated_rows)


def item_scores(result, cand_rows):
    length_out = jnp.sqrt(jnp.sum(result * result, -1, keepdims=True) + epsilon)
    single_output = result / length_out
    row_float = cand_rows.astype(jnp.float32)
    row_length = jnp.sqrt(jnp.sum(row_float * row_float, -1, keepdims=True) + epsilon)
    single_row = row_float / row_length
    logit_values = jnp.sum(single_output[:, None, :] * single_row, -1) / softmax_warmth
    exponent = jnp.exp(logit_values)
    softmax_weights = exponent / jnp.sum(exponent, -1, keepdims=True)
    logit_gradient = softmax_weights - (jnp.arange(NCAND) == 0).astype(jnp.float32)[None, :]
    gathered_rows = jnp.sum(logit_gradient[..., None] * single_row, 1) / softmax_warmth
    upstream = (
        gathered_rows - single_output * jnp.sum(single_output * gathered_rows, -1, keepdims=True)
    ) / length_out
    scattered_rows = logit_gradient[..., None] * single_output[:, None, :] / softmax_warmth
    grad_rows = (
        (scattered_rows - single_row * jnp.sum(single_row * scattered_rows, -1, keepdims=True))
        / row_length
    ).astype(jnp.bfloat16)
    return (upstream, grad_rows)


def body(events, lengths, destinations, history, negatives, in_weight, out_weight, item_table):
    owners = lax.axis_size("seq")
    hidden_width = out_weight.shape[1]
    tok_rows = events.shape[0]
    slot_rows = 3 * tok_rows // (2 * owners)
    user_lengths = lengths[0]
    user_dests = destinations[0]
    starts = jnp.cumsum(user_lengths) - user_lengths
    candidates = jnp.concatenate([history[:, None], negatives], 1)
    chosen_user = (user_dests[None, :] == jnp.arange(owners)[:, None]).astype(jnp.int32)
    send_length = jnp.sum(chosen_user * user_lengths[None, :], 1)
    send_start = jnp.sum(chosen_user * starts[None, :], 1)
    slot_index = jnp.arange(slot_rows)
    filled = slot_index[None, :] < send_length[:, None]
    sources = jnp.clip(send_start[:, None] + slot_index[None, :], 0, tok_rows - 1)
    send_tokens = jnp.where(filled[..., None], events[sources], jnp.zeros((), jnp.bfloat16))
    send_items = jnp.where(filled[..., None], candidates[sources], 0)
    got_tokens, got_items, got_length = (
        lax.all_to_all(send_tokens, "seq", split_axis=0, concat_axis=0, tiled=True),
        lax.all_to_all(send_items, "seq", split_axis=0, concat_axis=0, tiled=True),
        lax.all_to_all(send_length[:, None], "seq", split_axis=0, concat_axis=0, tiled=True),
    )
    counts = got_length[:, 0]
    block_ends = jnp.cumsum(counts)
    offsets = block_ends - counts
    positions = jnp.arange(tok_rows)
    anchor = jnp.minimum(
        jnp.sum((block_ends[None, :] <= positions[:, None]).astype(jnp.int32), 1), owners - 1
    )
    placed = anchor * slot_rows + positions - offsets[anchor]
    slot_tokens = got_tokens.reshape(owners * slot_rows, D)
    relayed_items = got_items.reshape(owners * slot_rows, NCAND)[placed]
    attend_mask = (
        (anchor[:, None] == anchor[None, :]) & (positions[None, :] <= positions[:, None])
    ).astype(jnp.float32)[None]
    batch_count = 1
    result_rows, saved_state = layer_forward(
        slot_tokens[placed], attend_mask, in_weight, out_weight, batch_count
    )
    per_owner = tok_rows * NCAND // owners
    flat_items = relayed_items.reshape(-1)
    owner_order = jnp.argsort(flat_items // VOCAB_DEV, stable=True)
    asked_rows = (flat_items % VOCAB_DEV)[owner_order].reshape(owners, per_owner)
    requested = lax.all_to_all(asked_rows, "seq", split_axis=0, concat_axis=0, tiled=True)
    found_rows = item_table[requested]
    fetched, requested = (
        lax.all_to_all(found_rows, "seq", split_axis=0, concat_axis=0, tiled=True),
        requested,
    )
    cand_rows = (
        jnp.zeros((tok_rows * NCAND, D), jnp.bfloat16)
        .at[owner_order]
        .set(fetched.reshape(-1, D))
        .reshape(tok_rows, NCAND, D)
    )
    upstream, grad_rows = item_scores(result_rows, cand_rows)
    outgoing = grad_rows.reshape(-1, D)[owner_order].reshape(owners, per_owner, D)
    returned = lax.all_to_all(outgoing, "seq", split_axis=0, concat_axis=0, tiled=True)
    table_part = jax.ops.segment_sum(
        returned.reshape(-1, D).astype(jnp.float32), requested.reshape(-1), num_segments=VOCAB_DEV
    )
    normed_in, grad_preact, upstream_b, gated_rows = layer_backward(
        upstream, saved_state, attend_mask, out_weight, batch_count
    )
    first_term = lax.dot_general(
        lax.slice_in_dim(normed_in, 0, lax.axis_size("seq") * (D // owners), axis=1),
        grad_preact,
        (((0,), (0,)), ((), ())),
        preferred_element_type=jnp.float32,
    )
    second_term = lax.dot_general(
        lax.slice_in_dim(upstream_b, 0, lax.axis_size("seq") * (D // owners), axis=1),
        gated_rows,
        (((0,), (0,)), ((), ())),
        preferred_element_type=jnp.float32,
    )
    weight_shard = lax.psum_scatter(
        jnp.concatenate([first_term, second_term], 1).astype(jnp.bfloat16),
        "seq",
        scatter_dimension=0,
        tiled=True,
    ).astype(jnp.float32)
    table_grad, weight_shard = (
        lax.psum(table_part.astype(jnp.bfloat16), "grp").astype(jnp.float32),
        lax.psum(weight_shard.astype(jnp.bfloat16), "grp").astype(jnp.float32),
    )
    layer_out = result_rows.astype(jnp.bfloat16)
    return (
        layer_out,
        weight_shard[:, : 4 * hidden_width],
        weight_shard[:, 4 * hidden_width :],
        table_grad,
    )


def solution(mesh):
    return jax.shard_map(
        body,
        mesh=mesh,
        in_specs=(
            P(("grp", "seq"), None),
            P(("grp", "seq"), None),
            P(("grp", "seq"), None),
            P(("grp", "seq")),
            P(("grp", "seq"), None),
            P(),
            P(),
            P("seq", None),
        ),
        out_specs=(P(("grp", "seq"), None), P("seq", None), P("seq", None), P("seq", None)),
        check_vma=False,
    )
```

profile of v0, /device:TPU:32, one launch (start us, length us, event | category | flops | bytes accessed | tf_op | source)
XLA Modules:
  0.0 399.3 jit_solution(15326774801198506185)
XLA Ops:
  10.3 8.6 %all-to-all-start.1 = ((s32[16,1,1]{2,1,0:T(1,128)}), s32[16,1,1]{2,1,0:T(1,128)S(1)}, u32[]{:S(2)}, u32[]{:S(2)}) async-start(s32[16,1,1]{2,1,0:T(1,128)} %copy.95), calls=%async_computation.1 | async-start | bytes 16384 | tf_op jit(solution)/shard_map/all_to_all | solution.py:191
  21.9 2.1 gather_fusion
  25.0 6.2 %all-to-all-start.2 = ((s32[16,24,4]{1,2,0:T(4,128)}), s32[16,24,4]{1,2,0:T(4,128)S(1)}, u32[]{:S(2)}, u32[]{:S(2)}) async-start(s32[16,24,4]{1,2,0:T(4,128)} %broadcast_select_fusion.1), calls=%async_computation.2 | async-start | bytes 65536 | tf_op jit(solution)/shard_map/all_to_all | solution.py:190
  32.6 4.3 %compare_select_fusion.5 = (s32[256,1]{0,1:T(1,128)S(1)}, s32[256,1]{0,1:T(1,128)S(1)}) fusion(s32[]{:T(128)} %bitcast.17, s32[]{:T(128)} %bitcast.18, s32[]{:T(128)} %bitcast.19, s32[]{:T(128)} %bitcast.20, s32[]{:T(128)} %bitcast.21, s32[]{:T(128)} %bitcast.23, s32[]{:T(128)} %bitcast.22, s32[256,1]{0,1:T(1,128)S(1)} %bitcast.229), kind=kLoop, calls=%fused_computation.155 | loop fusion | flops 3840 | bytes 3100 | tf_op jit(solution)/shard_map/gather | solution.py:200
  37.0 5.7 %select_select_fusion = s32[256]{0:T(256)S(1)} fusion(pred[256]{0:T(512)(128)(4,1)S(1)} %get-tuple-element.16, pred[256]{0:T(512)(128)(4,1)S(1)} %get-tuple-element.15, pred[256]{0:T(512)(128)(4,1)S(1)} %get-tuple-element.14, pred[256]{0:T(512)(128)(4,1)S(1)} %get-tuple-element.13, pred[256]{0:T(512)(128)(4,1)S(1)} %get-tuple-element.12, ...), kind=kLoop, calls=%fused_computation.165 | loop fusion | flops 2304 | bytes 4388 | tf_op jit(solution)/shard_map/gather | solution.py:200
  43.8 4.4 %sort.17 = (s32[1024]{0:T(1024)}, s32[1024]{0:T(1024)S(1)}) sort(s32[1024]{0:T(1024)S(1)} %get-tuple-element.33, s32[1024]{0:T(1024)S(1)} %iota.37), dimensions={0}, to_apply=%region_13.14 | sort | flops 10240 | bytes 16384 | tf_op jit(solution)/shard_map/jit(argsort)/sort | solution.py:212
  48.2 4.5 %gather_fusion.4 = s32[1024]{0:T(1024)S(1)} fusion(s32[1024]{0:T(1024)S(1)} %get-tuple-element.32, s32[1024]{0:T(1024)S(1)} %get-tuple-element.30), kind=kCustom, calls=%fused_computation.4 | custom fusion | bytes 12288 | tf_op jit(solution)/shard_map/gather | solution.py:213
  53.4 7.2 %all-to-all-start.3 = ((s32[16,1,64]{2,1,0:T(1,128)}), s32[16,1,64]{2,1,0:T(1,128)S(1)}, u32[]{:S(2)}, u32[]{:S(2)}) async-start(s32[16,1,64]{2,1,0:T(1,128)} %all_to_all.30), calls=%async_computation.3 | async-start | bytes 16384 | tf_op jit(solution)/shard_map/all_to_all | solution.py:214
  61.6 5.1 %all-to-all-done.3 = s32[16,1,64]{2,1,0:T(1,128)S(1)} async-done(((s32[16,1,64]{2,1,0:T(1,128)}), s32[16,1,64]{2,1,0:T(1,128)S(1)}, u32[]{:S(2)}, u32[]{:S(2)}) %all-to-all-start.3) | async-done | bytes 4128 | tf_op jit(solution)/shard_map/all_to_all | solution.py:214
  66.8 4.9 %all-to-all-start = ((bf16[16,24,1024]{2,1,0:T(8,128)(2,1)}), bf16[16,24,1024]{2,1,0:T(8,128)(2,1)S(1)}, u32[]{:S(2)}, u32[]{:S(2)}) async-start(bf16[16,24,1024]{2,1,0:T(8,128)(2,1)} %broadcast_select_fusion), calls=%async_computation | async-start | bytes 1572864 | tf_op jit(solution)/shard_map/all_to_all | solution.py:189
  72.2 5.4 %gather_fusion.5 = bf16[1024,1024]{1,0:T(8,128)(2,1)} fusion(bf16[512,1024]{1,0:T(8,128)(2,1)S(1)} %copy-done, s32[1024]{0:T(1024)S(1)} %broadcast_clamp_fusion), kind=kCustom, calls=%fused_computation.5 | custom fusion | bytes 4198400 | tf_op jit(solution)/shard_map/gather | solution.py:215
  77.6 13.0 %all-to-all-done = bf16[16,24,1024]{2,1,0:T(8,128)(2,1)S(1)} async-done(((bf16[16,24,1024]{2,1,0:T(8,128)(2,1)}), bf16[16,24,1024]{2,1,0:T(8,128)(2,1)S(1)}, u32[]{:S(2)}, u32[]{:S(2)}) %all-to-all-start) | async-done | bytes 786464 | tf_op jit(solution)/shard_map/all_to_all | solution.py:189
  90.6 6.9 %all-to-all-start.4 = ((bf16[16,64,1024]{2,1,0:T(8,128)(2,1)}), bf16[16,64,1024]{2,1,0:T(8,128)(2,1)}, u32[]{:S(2)}, u32[]{:S(2)}) async-start(bf16[16,64,1024]{2,1,0:T(8,128)(2,1)} %bitcast.201), calls=%async_computation.4 | async-start | bytes 4194304 | tf_op jit(solution)/shard_map/all_to_all | solution.py:217
  99.4 4.9 %multiply_convert_fusion = (bf16[256,2048]{1,0:T(8,128)(2,1)S(1)}, f32[256,2048]{1,0:T(8,128)}) fusion(bf16[1024,2048]{1,0:T(8,128)(2,1)} %param.13, bf16[256,1024]{1,0:T(8,128)(2,1)S(1)} %gather_fusion.1, f32[256]{0:T(256)S(1)} %add_rsqrt_fusion.1, f32[256]{0:T(256)S(1)} %broadcast_multiply_fusion.2), kind=kOutput, calls=%fused_computation.22 | convolution fusion | flops 1077411840 | bytes 7866368 | tf_op jit(solution)/shard_map/dot_general | solution.py:36
  110.4 3.1 mul.315
  113.6 5.4 %mul.316 = f32[1024,1024]{1,0:T(8,128)} reshape(f32[256,4,1024]{2,1,0:T(4,128)} %mul.315) | data formatting | bytes 8388608 | tf_op jit(solution)/shard_map/mul | solution.py:155
  118.9 25.8 %all-to-all-done.4 = bf16[16,64,1024]{2,1,0:T(8,128)(2,1)} async-done(((bf16[16,64,1024]{2,1,0:T(8,128)(2,1)}), bf16[16,64,1024]{2,1,0:T(8,128)(2,1)}, u32[]{:S(2)}, u32[]{:S(2)}) %all-to-all-start.4) | async-done | bytes 2097184 | tf_op jit(solution)/shard_map/all_to_all | solution.py:217
  144.7 6.8 %scatter_custom_fusion = bf16[1024,1024]{1,0:T(8,128)(2,1)S(1)} fusion(s32[1024]{0:T(1024)S(1)} %get-tuple-element.31, bf16[1024,1024]{1,0:T(8,128)(2,1)} %bitcast.52, bf16[]{:T(256)} %constant.83.clone.1), kind=kCustom, calls=%fused_computation.67 | custom fusion | bytes 2097664 | tf_op jit(solution)/shard_map/scatter | solution.py:223
  152.0 3.0 reshape.577
  155.8 2.9 multiply_reduce_fusion.2
  163.4 4.6 %multiply_reduce_fusion.1 = f32[256,1024]{1,0:T(8,128)S(1)} fusion(f32[256,4,1024]{2,1,0:T(4,128)} %reshape.577, f32[256,4]{1,0:T(8,128)} %sqrt.22, f32[256,4]{1,0:T(8,128)S(1)} %divide_subtract_fusion), kind=kLoop, calls=%fused_computation.15 | loop fusion | flops 2883584 | bytes 5251072 | tf_op jit(solution)/shard_map/reduce_sum | solution.py:159
  179.0 2.7 pad_maximum_fusion
  182.8 3.3 multiply_reduce_fusion
  186.2 2.6 divide_convert_fusion
  188.8 5.3 %gather_fusion.6 = bf16[1024,1024]{1,0:T(8,128)(2,1)} fusion(bf16[1024,1024]{1,0:T(8,128)(2,1)S(1)} %divide_convert_fusion, s32[1024]{0:T(1024)S(1)} %copy-done.34), kind=kCustom, calls=%fused_computation.6 | custom fusion | bytes 4198400 | tf_op jit(solution)/shard_map/gather | solution.py:227
  194.1 6.8 %all-to-all-start.5 = ((bf16[16,64,1024]{2,1,0:T(8,128)(2,1)}), bf16[16,64,1024]{2,1,0:T(8,128)(2,1)S(1)}, u32[]{:S(2)}, u32[]{:S(2)}) async-start(bf16[16,64,1024]{2,1,0:T(8,128)(2,1)} %bitcast.202), calls=%async_computation.6 | async-start | bytes 4194304 | tf_op jit(solution)/shard_map/all_to_all | solution.py:228
  202.5 55.5 %all-to-all-done.5 = bf16[16,64,1024]{2,1,0:T(8,128)(2,1)S(1)} async-done(((bf16[16,64,1024]{2,1,0:T(8,128)(2,1)}), bf16[16,64,1024]{2,1,0:T(8,128)(2,1)S(1)}, u32[]{:S(2)}, u32[]{:S(2)}) %all-to-all-start.5) | async-done | bytes 2097184 | tf_op jit(solution)/shard_map/all_to_all | solution.py:228
  258.0 10.4 %scatter_custom_fusion.1 = f32[512,1024]{1,0:T(8,128)} fusion(s32[1024]{0:T(1024)S(1)} %reshape.668, bf16[1024,1024]{1,0:T(8,128)(2,1)S(1)} %bitcast.203, f32[]{:T(128)} %constant.88.clone.1), kind=kCustom, calls=%fused_computation.10 | custom fusion | flops 2097152 | bytes 4194308 | tf_op jit(solution)/shard_map/scatter-add | solution.py:229
  268.4 2.8 convert_element_type.134
  271.2 11.9 %reduce-scatter.2.cloned.1.call-done = bf16[64,2560]{1,0:T(8,128)(2,1)} async-done(((bf16[1024,2560]{1,0:T(8,128)(2,1)}), bf16[64,2560]{1,0:T(8,128)(2,1)}) %reduce-scatter.2.cloned.1.call-update) | async-done | bytes 327696 | tf_op jit(solution)/shard_map/reduce_scatter | solution.py:247
  283.1 103.2 %all-reduce.3.cloned.1.call-done = (bf16[64,2560]{1,0:T(8,128)(2,1)}, bf16[512,1024]{1,0:T(8,128)(2,1)}) async-done(((bf16[64,2560]{1,0:T(8,128)(2,1)}, bf16[512,1024]{1,0:T(8,128)(2,1)}), (bf16[64,2560]{1,0:T(8,128)(2,1)}, bf16[512,1024]{1,0:T(8,128)(2,1)})) %all-reduce.3.cloned.1.call-update) | async-done | bytes 1376272 | tf_op jit(solution)/shard_map/psum | solution.py:255
  389.7 2.8 convert_element_type.135
  (212 shorter events, 42.2 us)
Async XLA Ops:
  7.2 65.1 %copy-start = (bf16[512,1024]{1,0:T(8,128)(2,1)S(1)}, bf16[512,1024]{1,0:T(8,128)(2,1)}, u32[]{:S(2)}) copy-start(bf16[512,1024]{1,0:T(8,128)(2,1)} %param.15) | copy-start | bytes 3145732
  7.2 14.7 %copy-start.3 = (bf16[256,1024]{1,0:T(8,128)(2,1)S(1)}, bf16[256,1024]{1,0:T(8,128)(2,1)}, u32[]{:S(2)}) copy-start(bf16[256,1024]{1,0:T(8,128)(2,1)} %param.8) | copy-start | bytes 1572868
  10.3 14.7 %all-to-all-start.1 = ((s32[16,1,1]{2,1,0:T(1,128)}), s32[16,1,1]{2,1,0:T(1,128)S(1)}, u32[]{:S(2)}, u32[]{:S(2)}) async-start(s32[16,1,1]{2,1,0:T(1,128)} %copy.95), calls=%async_computation.1 | async-start | bytes 16384 | tf_op jit(solution)/shard_map/all_to_all | solution.py:191
  25.0 17.7 %all-to-all-start.2 = ((s32[16,24,4]{1,2,0:T(4,128)}), s32[16,24,4]{1,2,0:T(4,128)S(1)}, u32[]{:S(2)}, u32[]{:S(2)}) async-start(s32[16,24,4]{1,2,0:T(4,128)} %broadcast_select_fusion.1), calls=%async_computation.2 | async-start | bytes 65536 | tf_op jit(solution)/shard_map/all_to_all | solution.py:190
  32.6 72.4 %copy-start.40 = (s32[256]{0:T(256)}, s32[256]{0:T(256)S(1)}, u32[]{:S(2)}) copy-start(s32[256]{0:T(256)S(1)} %broadcast_minimum_fusion) | copy-start | bytes 3076
  48.2 4.5 %copy-start.33 = (s32[1024]{0:T(1024)}, s32[1024]{0:T(1024)S(1)}, u32[]{:S(2)}) copy-start(s32[1024]{0:T(1024)S(1)} %get-tuple-element.30) | copy-start | bytes 12292
  53.4 13.4 %all-to-all-start.3 = ((s32[16,1,64]{2,1,0:T(1,128)}), s32[16,1,64]{2,1,0:T(1,128)S(1)}, u32[]{:S(2)}, u32[]{:S(2)}) async-start(s32[16,1,64]{2,1,0:T(1,128)} %all_to_all.30), calls=%async_computation.3 | async-start | bytes 16384 | tf_op jit(solution)/shard_map/all_to_all | solution.py:214
  66.8 23.8 %all-to-all-start = ((bf16[16,24,1024]{2,1,0:T(8,128)(2,1)}), bf16[16,24,1024]{2,1,0:T(8,128)(2,1)S(1)}, u32[]{:S(2)}, u32[]{:S(2)}) async-start(bf16[16,24,1024]{2,1,0:T(8,128)(2,1)} %broadcast_select_fusion), calls=%async_computation | async-start | bytes 1572864 | tf_op jit(solution)/shard_map/all_to_all | solution.py:189
  90.6 54.1 %all-to-all-start.4 = ((bf16[16,64,1024]{2,1,0:T(8,128)(2,1)}), bf16[16,64,1024]{2,1,0:T(8,128)(2,1)}, u32[]{:S(2)}, u32[]{:S(2)}) async-start(bf16[16,64,1024]{2,1,0:T(8,128)(2,1)} %bitcast.201), calls=%async_computation.4 | async-start | bytes 4194304 | tf_op jit(solution)/shard_map/all_to_all | solution.py:217
  97.5 185.5 %reduce-scatter.2.cloned.1.call-start = ((), (), s32[]{:S(2)}) async-start(), calls=%async_computation.7 | async-start | bytes 5570560 | tf_op jit(solution)/shard_map/reduce_scatter | solution.py:247
  98.9 8.7 %copy-start.5 = (bf16[256,1024]{1,0:T(8,128)(2,1)}, bf16[256,1024]{1,0:T(8,128)(2,1)S(1)}, u32[]{:S(2)}) copy-start(bf16[256,1024]{1,0:T(8,128)(2,1)S(1)} %gather_fusion.1) | copy-start | bytes 1572868
  99.1 5.2 %copy-start.42 = (f32[256]{0:T(256)}, f32[256]{0:T(256)S(1)}, u32[]{:S(2)}) copy-start(f32[256]{0:T(256)S(1)} %broadcast_multiply_fusion.2) | copy-start | bytes 3076
  99.4 4.9 %copy-start.47 = (f32[256]{0:T(256)}, f32[256]{0:T(256)S(1)}, u32[]{:S(2)}) copy-start(f32[256]{0:T(256)S(1)} %add_rsqrt_fusion.1) | copy-start | bytes 3076
  104.3 3.3 copy-start.17
  104.4 2.7 copy-start.15
  106.0 3.5 copy-start.19
  106.0 3.5 copy-start.21
  106.0 3.5 copy-start.23
  106.0 3.5 copy-start.25
  106.7 2.8 copy-start.9
  107.0 2.5 copy-start.11
  107.4 2.1 copy-start.13
  107.4 2.1 copy-start.36
  107.6 1.9 copy-start.44
  109.5 4.0 %copy-start.38 = (f32[256]{0:T(256)}, f32[256]{0:T(256)S(1)}, u32[]{:S(2)}) copy-start(f32[256]{0:T(256)S(1)} %add_sqrt_fusion.1) | copy-start | bytes 3076
  151.5 31.2 %copy-start.2 = (bf16[1024,1024]{1,0:T(8,128)(2,1)}, bf16[1024,1024]{1,0:T(8,128)(2,1)S(1)}, u32[]{:S(2)}) copy-start(bf16[1024,1024]{1,0:T(8,128)(2,1)S(1)} %scatter_custom_fusion) | copy-start | bytes 6291460
  175.7 1.8 copy-start.51
  182.8 3.5 copy-start.4
  186.2 2.6 copy-start.34
  194.1 63.8 %all-to-all-start.5 = ((bf16[16,64,1024]{2,1,0:T(8,128)(2,1)}), bf16[16,64,1024]{2,1,0:T(8,128)(2,1)S(1)}, u32[]{:S(2)}, u32[]{:S(2)}) async-start(bf16[16,64,1024]{2,1,0:T(8,128)(2,1)} %bitcast.202), calls=%async_computation.6 | async-start | bytes 4194304 | tf_op jit(solution)/shard_map/all_to_all | solution.py:228
  200.9 185.4 %all-reduce.3.cloned.1.call-start = ((), (), s32[]{:S(2)}) async-start(), calls=%async_computation.8 | async-start | bytes 2752512 | tf_op jit(solution)/shard_map/psum | solution.py:255
  386.3 6.2 %copy-start.1 = (bf16[512,1024]{1,0:T(8,128)(2,1)S(1)}, bf16[512,1024]{1,0:T(8,128)(2,1)}, u32[]{:S(2)}) copy-start(bf16[512,1024]{1,0:T(8,128)(2,1)} %param.15) | copy-start | bytes 3145732
  (28 other events, 33.1 us)
Sparse Core Ops, SparseCore 0:
  181.9 101.0 reduce-scatter.1
  286.4 99.8 all-reduce.2
where the time goes:
time: 401 us; the launch traced here: 399 us
  waiting for transfers between devices  216 us (54%)
  other arithmetic  59.3 us (15%)
  local copies, waits for them, and re-layouts  53.1 us (13%)
  starting transfers between devices  41.1 us (10%)
  matrix products  15.2 us (4%)
  between operations  15.1 us (4%)
    psum x1, waiting for transfers between devices, body(): lax.psum(weight_shard.astype(jnp.bfloat16), 'grp').astype(jnp.float32)  103 us
    all_to_all x1, waiting for transfers between devices, body(): lax.all_to_all(outgoing, 'seq', split_axis=0, concat_axis=0, tiled=True)  55.5 us
    all_to_all x1, waiting for transfers between devices, body(): lax.all_to_all(found_rows, 'seq', split_axis=0, concat_axis=0, tiled=True)  25.8 us
    all_to_all x1, waiting for transfers between devices, body(): lax.all_to_all(send_tokens, 'seq', split_axis=0, concat_axis=0, tiled=True)  13 us
    reduce_scatter x1, waiting for transfers between devices, body(): lax.psum_scatter(jnp.concatenate([first_term, second_term], 1).astype(jnp...  11.9 us
    scatter-add x1, other arithmetic, body(): jax.ops.segment_sum(returned.reshape(-1, D).astype(jnp.float32), requeste...  10.4 us
    gather x3, other arithmetic, body(): placed = anchor * slot_rows + positions - offsets[anchor]  10.1 us
    all_to_all x1, starting transfers between devices, body(): lax.all_to_all(send_length[:, None], 'seq', split_axis=0, concat_axis=0,...  8.59 us
  transfers between devices with their start and end apart: 8, of which 7 were waited for; matrix products, arithmetic and copies ran while one was open for 18% of the time, Pallas kernels for 0%

commit v1 on v0

--- a/solution.py
+++ b/solution.py
@@ -252,7 +252,9 @@
     ).astype(jnp.float32)
     table_grad, weight_shard = (
         lax.psum(table_part.astype(jnp.bfloat16), "grp").astype(jnp.float32),
-        lax.psum(weight_shard.astype(jnp.bfloat16), "grp").astype(jnp.float32),
+        jnp.sum(lax.all_gather(weight_shard.astype(jnp.bfloat16), "grp"), axis=0).astype(
+            jnp.float32
+        ),
     )
     layer_out = result_rows.astype(jnp.bfloat16)
     return (

time: 401 us -> 448 us (1.12)
  waiting for transfers between devices: 216 us -> 259 us
    all_gather x0 -> x1, waiting for transfers between devices: none -> 59.9 us  [body(): lax.all_gather(weight_shard.astype(jnp.bfloat16), 'grp')]
    psum x1, waiting for transfers between devices: 103 us -> 86.9 us  [body(): lax.psum(table_part.astype(jnp.bfloat16), 'grp').astype(jnp.float32)]
  transfers between devices with their start and end apart: 8 -> 9, of which waited for: 7 -> 8; matrix products, arithmetic and copies ran while one was open for 18% -> 16% of each run, Pallas kernels for 0% -> 0%
where the time goes in v1:
time: 448 us; the launch traced here: 446 us
  waiting for transfers between devices  259 us (58%)
  other arithmetic  62.6 us (14%)
  local copies, waits for them, and re-layouts  51.2 us (11%)
  starting transfers between devices  41.2 us (9%)
  between operations  16.5 us (4%)
  matrix products  15.2 us (3%)
    psum x1, waiting for transfers between devices, body(): lax.psum(table_part.astype(jnp.bfloat16), 'grp').astype(jnp.float32)  86.9 us
    all_gather x1, waiting for transfers between devices, body(): lax.all_gather(weight_shard.astype(jnp.bfloat16), 'grp')  59.9 us
    all_to_all x1, waiting for transfers between devices, body(): lax.all_to_all(outgoing, 'seq', split_axis=0, concat_axis=0, tiled=True)  55.5 us
    all_to_all x1, waiting for transfers between devices, body(): lax.all_to_all(found_rows, 'seq', split_axis=0, concat_axis=0, tiled=True)  25.8 us
    all_to_all x1, waiting for transfers between devices, body(): lax.all_to_all(send_tokens, 'seq', split_axis=0, concat_axis=0, tiled=True)  13 us
    reduce_scatter x1, waiting for transfers between devices, body(): lax.psum_scatter(jnp.concatenate([first_term, second_term], 1).astype(jnp...  11.8 us
    scatter-add x1, other arithmetic, body(): jax.ops.segment_sum(returned.reshape(-1, D).astype(jnp.float32), requeste...  10.4 us
    gather x3, other arithmetic, body(): placed = anchor * slot_rows + positions - offsets[anchor]  10.1 us
  transfers between devices with their start and end apart: 9, of which 8 were waited for; matrix products, arithmetic and copies ran while one was open for 16% of the time, Pallas kernels for 0%

profile of v1, /device:TPU:32, one launch (start us, length us, event | category | flops | bytes accessed | tf_op | source)
XLA Modules:
  0.0 445.8 jit_solution(17509701312399798320)
XLA Ops:
  11.1 8.6 %all-to-all-start.1 = ((s32[16,1,1]{2,1,0:T(1,128)}), s32[16,1,1]{2,1,0:T(1,128)S(1)}, u32[]{:S(2)}, u32[]{:S(2)}) async-start(s32[16,1,1]{2,1,0:T(1,128)} %copy.95), calls=%async_computation.1 | async-start | bytes 16384 | tf_op jit(solution)/shard_map/all_to_all | solution.py:191
  25.8 6.2 %all-to-all-start.2 = ((s32[16,24,4]{1,2,0:T(4,128)}), s32[16,24,4]{1,2,0:T(4,128)S(1)}, u32[]{:S(2)}, u32[]{:S(2)}) async-start(s32[16,24,4]{1,2,0:T(4,128)} %broadcast_select_fusion.1), calls=%async_computation.2 | async-start | bytes 65536 | tf_op jit(solution)/shard_map/all_to_all | solution.py:190
  33.4 4.3 compare_select_fusion.5
  37.8 5.7 %select_select_fusion = s32[256]{0:T(256)S(1)} fusion(pred[256]{0:T(512)(128)(4,1)S(1)} %get-tuple-element.16, pred[256]{0:T(512)(128)(4,1)S(1)} %get-tuple-element.15, pred[256]{0:T(512)(128)(4,1)S(1)} %get-tuple-element.14, pred[256]{0:T(512)(128)(4,1)S(1)} %get-tuple-element.13, pred[256]{0:T(512)(128)(4,1)S(1)} %get-tuple-element.12, ...), kind=kLoop, calls=%fused_computation.165 | loop fusion | flops 2304 | bytes 4388 | tf_op jit(solution)/shard_map/gather | solution.py:200
  44.6 4.4 sort.17
  49.0 4.5 %gather_fusion.4 = s32[1024]{0:T(1024)S(1)} fusion(s32[1024]{0:T(1024)S(1)} %get-tuple-element.30, s32[1024]{0:T(1024)S(1)} %get-tuple-element.28), kind=kCustom, calls=%fused_computation.4 | custom fusion | bytes 12288 | tf_op jit(solution)/shard_map/gather | solution.py:213
  54.2 7.2 %all-to-all-start.3 = ((s32[16,1,64]{2,1,0:T(1,128)}), s32[16,1,64]{2,1,0:T(1,128)S(1)}, u32[]{:S(2)}, u32[]{:S(2)}) async-start(s32[16,1,64]{2,1,0:T(1,128)} %all_to_all.30), calls=%async_computation.3 | async-start | bytes 16384 | tf_op jit(solution)/shard_map/all_to_all | solution.py:214
  62.4 5.1 %all-to-all-done.3 = s32[16,1,64]{2,1,0:T(1,128)S(1)} async-done(((s32[16,1,64]{2,1,0:T(1,128)}), s32[16,1,64]{2,1,0:T(1,128)S(1)}, u32[]{:S(2)}, u32[]{:S(2)}) %all-to-all-start.3) | async-done | bytes 4128 | tf_op jit(solution)/shard_map/all_to_all | solution.py:214
  67.6 4.9 %all-to-all-start = ((bf16[16,24,1024]{2,1,0:T(8,128)(2,1)}), bf16[16,24,1024]{2,1,0:T(8,128)(2,1)S(1)}, u32[]{:S(2)}, u32[]{:S(2)}) async-start(bf16[16,24,1024]{2,1,0:T(8,128)(2,1)} %broadcast_select_fusion), calls=%async_computation | async-start | bytes 1572864 | tf_op jit(solution)/shard_map/all_to_all | solution.py:189
  73.1 5.4 %gather_fusion.5 = bf16[1024,1024]{1,0:T(8,128)(2,1)} fusion(bf16[512,1024]{1,0:T(8,128)(2,1)S(1)} %copy-done, s32[1024]{0:T(1024)S(1)} %broadcast_clamp_fusion), kind=kCustom, calls=%fused_computation.5 | custom fusion | bytes 4198400 | tf_op jit(solution)/shard_map/gather | solution.py:215
  78.4 13.0 %all-to-all-done = bf16[16,24,1024]{2,1,0:T(8,128)(2,1)S(1)} async-done(((bf16[16,24,1024]{2,1,0:T(8,128)(2,1)}), bf16[16,24,1024]{2,1,0:T(8,128)(2,1)S(1)}, u32[]{:S(2)}, u32[]{:S(2)}) %all-to-all-start) | async-done | bytes 786464 | tf_op jit(solution)/shard_map/all_to_all | solution.py:189
  91.4 6.9 %all-to-all-start.4 = ((bf16[16,64,1024]{2,1,0:T(8,128)(2,1)}), bf16[16,64,1024]{2,1,0:T(8,128)(2,1)}, u32[]{:S(2)}, u32[]{:S(2)}) async-start(bf16[16,64,1024]{2,1,0:T(8,128)(2,1)} %bitcast.202), calls=%async_computation.4 | async-start | bytes 4194304 | tf_op jit(solution)/shard_map/all_to_all | solution.py:217
  100.2 4.9 %multiply_convert_fusion = (bf16[256,2048]{1,0:T(8,128)(2,1)S(1)}, f32[256,2048]{1,0:T(8,128)}) fusion(bf16[1024,2048]{1,0:T(8,128)(2,1)} %param.13, bf16[256,1024]{1,0:T(8,128)(2,1)S(1)} %gather_fusion.1, f32[256]{0:T(256)S(1)} %add_rsqrt_fusion.1, f32[256]{0:T(256)S(1)} %broadcast_multiply_fusion.2), kind=kOutput, calls=%fused_computation.22 | convolution fusion | flops 1077411840 | bytes 7866368 | tf_op jit(solution)/shard_map/dot_general | solution.py:36
  111.3 3.1 mul.315
  114.4 5.4 %mul.316 = f32[1024,1024]{1,0:T(8,128)} reshape(f32[256,4,1024]{2,1,0:T(4,128)} %mul.315) | data formatting | bytes 8388608 | tf_op jit(solution)/shard_map/mul | solution.py:155
  119.8 25.8 %all-to-all-done.4 = bf16[16,64,1024]{2,1,0:T(8,128)(2,1)} async-done(((bf16[16,64,1024]{2,1,0:T(8,128)(2,1)}), bf16[16,64,1024]{2,1,0:T(8,128)(2,1)}, u32[]{:S(2)}, u32[]{:S(2)}) %all-to-all-start.4) | async-done | bytes 2097184 | tf_op jit(solution)/shard_map/all_to_all | solution.py:217
  145.5 6.8 %scatter_custom_fusion = bf16[1024,1024]{1,0:T(8,128)(2,1)S(1)} fusion(s32[1024]{0:T(1024)S(1)} %get-tuple-element.29, bf16[1024,1024]{1,0:T(8,128)(2,1)} %bitcast.52, bf16[]{:T(256)} %constant.84.clone.1), kind=kCustom, calls=%fused_computation.67 | custom fusion | bytes 2097664 | tf_op jit(solution)/shard_map/scatter | solution.py:223
  152.8 3.0 reshape.577
  156.7 2.9 multiply_reduce_fusion.2
  164.2 4.6 %multiply_reduce_fusion.1 = f32[256,1024]{1,0:T(8,128)S(1)} fusion(f32[256,4,1024]{2,1,0:T(4,128)} %reshape.577, f32[256,4]{1,0:T(8,128)} %sqrt.22, f32[256,4]{1,0:T(8,128)S(1)} %divide_subtract_fusion), kind=kLoop, calls=%fused_computation.15 | loop fusion | flops 2883584 | bytes 5251072 | tf_op jit(solution)/shard_map/reduce_sum | solution.py:159
  179.9 2.7 pad_maximum_fusion
  183.6 3.3 multiply_reduce_fusion
  189.6 5.3 %gather_fusion.6 = bf16[1024,1024]{1,0:T(8,128)(2,1)} fusion(bf16[1024,1024]{1,0:T(8,128)(2,1)S(1)} %divide_convert_fusion, s32[1024]{0:T(1024)S(1)} %copy-done.34), kind=kCustom, calls=%fused_computation.6 | custom fusion | bytes 4198400 | tf_op jit(solution)/shard_map/gather | solution.py:227
  195.0 6.8 %all-to-all-start.5 = ((bf16[16,64,1024]{2,1,0:T(8,128)(2,1)}), bf16[16,64,1024]{2,1,0:T(8,128)(2,1)S(1)}, u32[]{:S(2)}, u32[]{:S(2)}) async-start(bf16[16,64,1024]{2,1,0:T(8,128)(2,1)} %bitcast.203), calls=%async_computation.6 | async-start | bytes 4194304 | tf_op jit(solution)/shard_map/all_to_all | solution.py:228
  203.3 55.5 %all-to-all-done.5 = bf16[16,64,1024]{2,1,0:T(8,128)(2,1)S(1)} async-done(((bf16[16,64,1024]{2,1,0:T(8,128)(2,1)}), bf16[16,64,1024]{2,1,0:T(8,128)(2,1)S(1)}, u32[]{:S(2)}, u32[]{:S(2)}) %all-to-all-start.5) | async-done | bytes 2097184 | tf_op jit(solution)/shard_map/all_to_all | solution.py:228
  258.8 10.4 %scatter_custom_fusion.1 = f32[512,1024]{1,0:T(8,128)} fusion(s32[1024]{0:T(1024)S(1)} %reshape.668, bf16[1024,1024]{1,0:T(8,128)(2,1)S(1)} %bitcast.204, f32[]{:T(128)} %constant.89.clone.1), kind=kCustom, calls=%fused_computation.10 | custom fusion | flops 2097152 | bytes 4194308 | tf_op jit(solution)/shard_map/scatter-add | solution.py:229
  269.2 2.8 convert_element_type.136
  272.1 11.8 %reduce-scatter.2.cloned.1.call-done = bf16[64,2560]{1,0:T(8,128)(2,1)} async-done(((bf16[1024,2560]{1,0:T(8,128)(2,1)}), bf16[64,2560]{1,0:T(8,128)(2,1)}) %reduce-scatter.2.cloned.1.call-update) | async-done | bytes 327696 | tf_op jit(solution)/shard_map/reduce_scatter | solution.py:247
  283.9 86.9 %all-reduce.2.cloned.1.call-done = bf16[512,1024]{1,0:T(8,128)(2,1)} async-done(((bf16[512,1024]{1,0:T(8,128)(2,1)}), bf16[512,1024]{1,0:T(8,128)(2,1)}) %all-reduce.2.cloned.1.call-update) | async-done | bytes 1048592 | tf_op jit(solution)/shard_map/psum | solution.py:254
  370.8 2.8 convert_element_type.137
  373.6 59.9 %all-gather.3.cloned.1.call-done = bf16[1024,2560]{1,0:T(8,128)(2,1)} async-done(((bf16[64,2560]{1,0:T(8,128)(2,1)}), bf16[1024,2560]{1,0:T(8,128)(2,1)}) %all-gather.3.cloned.1.call-update) | async-done | bytes 5242896 | tf_op jit(solution)/shard_map/all_gather | solution.py:255
  433.5 3.3 reduce_sum.207
  (216 shorter events, 45.0 us)
Async XLA Ops:
  8.0 65.1 %copy-start = (bf16[512,1024]{1,0:T(8,128)(2,1)S(1)}, bf16[512,1024]{1,0:T(8,128)(2,1)}, u32[]{:S(2)}) copy-start(bf16[512,1024]{1,0:T(8,128)(2,1)} %param.15) | copy-start | bytes 3145732
  8.0 14.7 %copy-start.3 = (bf16[256,1024]{1,0:T(8,128)(2,1)S(1)}, bf16[256,1024]{1,0:T(8,128)(2,1)}, u32[]{:S(2)}) copy-start(bf16[256,1024]{1,0:T(8,128)(2,1)} %param.8) | copy-start | bytes 1572868
  11.1 14.7 %all-to-all-start.1 = ((s32[16,1,1]{2,1,0:T(1,128)}), s32[16,1,1]{2,1,0:T(1,128)S(1)}, u32[]{:S(2)}, u32[]{:S(2)}) async-start(s32[16,1,1]{2,1,0:T(1,128)} %copy.95), calls=%async_computation.1 | async-start | bytes 16384 | tf_op jit(solution)/shard_map/all_to_all | solution.py:191
  25.8 17.7 %all-to-all-start.2 = ((s32[16,24,4]{1,2,0:T(4,128)}), s32[16,24,4]{1,2,0:T(4,128)S(1)}, u32[]{:S(2)}, u32[]{:S(2)}) async-start(s32[16,24,4]{1,2,0:T(4,128)} %broadcast_select_fusion.1), calls=%async_computation.2 | async-start | bytes 65536 | tf_op jit(solution)/shard_map/all_to_all | solution.py:190
  33.4 72.4 %copy-start.40 = (s32[256]{0:T(256)}, s32[256]{0:T(256)S(1)}, u32[]{:S(2)}) copy-start(s32[256]{0:T(256)S(1)} %broadcast_minimum_fusion) | copy-start | bytes 3076
  49.0 4.5 %copy-start.33 = (s32[1024]{0:T(1024)}, s32[1024]{0:T(1024)S(1)}, u32[]{:S(2)}) copy-start(s32[1024]{0:T(1024)S(1)} %get-tuple-element.28) | copy-start | bytes 12292
  54.2 13.4 %all-to-all-start.3 = ((s32[16,1,64]{2,1,0:T(1,128)}), s32[16,1,64]{2,1,0:T(1,128)S(1)}, u32[]{:S(2)}, u32[]{:S(2)}) async-start(s32[16,1,64]{2,1,0:T(1,128)} %all_to_all.30), calls=%async_computation.3 | async-start | bytes 16384 | tf_op jit(solution)/shard_map/all_to_all | solution.py:214
  67.6 23.8 %all-to-all-start = ((bf16[16,24,1024]{2,1,0:T(8,128)(2,1)}), bf16[16,24,1024]{2,1,0:T(8,128)(2,1)S(1)}, u32[]{:S(2)}, u32[]{:S(2)}) async-start(bf16[16,24,1024]{2,1,0:T(8,128)(2,1)} %broadcast_select_fusion), calls=%async_computation | async-start | bytes 1572864 | tf_op jit(solution)/shard_map/all_to_all | solution.py:189
  91.4 54.1 %all-to-all-start.4 = ((bf16[16,64,1024]{2,1,0:T(8,128)(2,1)}), bf16[16,64,1024]{2,1,0:T(8,128)(2,1)}, u32[]{:S(2)}, u32[]{:S(2)}) async-start(bf16[16,64,1024]{2,1,0:T(8,128)(2,1)} %bitcast.202), calls=%async_computation.4 | async-start | bytes 4194304 | tf_op jit(solution)/shard_map/all_to_all | solution.py:217
  98.3 185.5 %reduce-scatter.2.cloned.1.call-start = ((), (), s32[]{:S(2)}) async-start(), calls=%async_computation.7 | async-start | bytes 5570560 | tf_op jit(solution)/shard_map/reduce_scatter | solution.py:247
  99.7 8.7 %copy-start.5 = (bf16[256,1024]{1,0:T(8,128)(2,1)}, bf16[256,1024]{1,0:T(8,128)(2,1)S(1)}, u32[]{:S(2)}) copy-start(bf16[256,1024]{1,0:T(8,128)(2,1)S(1)} %gather_fusion.1) | copy-start | bytes 1572868
  99.9 5.2 %copy-start.42 = (f32[256]{0:T(256)}, f32[256]{0:T(256)S(1)}, u32[]{:S(2)}) copy-start(f32[256]{0:T(256)S(1)} %broadcast_multiply_fusion.2) | copy-start | bytes 3076
  100.2 4.9 %copy-start.47 = (f32[256]{0:T(256)}, f32[256]{0:T(256)S(1)}, u32[]{:S(2)}) copy-start(f32[256]{0:T(256)S(1)} %add_rsqrt_fusion.1) | copy-start | bytes 3076
  105.1 3.3 copy-start.17
  105.2 2.7 copy-start.15
  106.8 3.5 copy-start.19
  106.8 3.5 copy-start.21
  106.8 3.5 copy-start.23
  106.8 3.5 copy-start.25
  107.5 2.8 copy-start.9
  107.8 2.5 copy-start.11
  108.2 2.1 copy-start.13
  108.2 2.1 copy-start.36
  108.5 1.9 copy-start.44
  110.4 4.0 copy-start.38
  152.3 31.2 %copy-start.2 = (bf16[1024,1024]{1,0:T(8,128)(2,1)}, bf16[1024,1024]{1,0:T(8,128)(2,1)S(1)}, u32[]{:S(2)}) copy-start(bf16[1024,1024]{1,0:T(8,128)(2,1)S(1)} %scatter_custom_fusion) | copy-start | bytes 6291460
  183.6 3.5 copy-start.4
  187.0 2.6 copy-start.34
  195.0 63.8 %all-to-all-start.5 = ((bf16[16,64,1024]{2,1,0:T(8,128)(2,1)}), bf16[16,64,1024]{2,1,0:T(8,128)(2,1)S(1)}, u32[]{:S(2)}, u32[]{:S(2)}) async-start(bf16[16,64,1024]{2,1,0:T(8,128)(2,1)} %bitcast.203), calls=%async_computation.6 | async-start | bytes 4194304 | tf_op jit(solution)/shard_map/all_to_all | solution.py:228
  201.7 169.1 %all-reduce.2.cloned.1.call-start = ((), (), s32[]{:S(2)}) async-start(), calls=%async_computation.8 | async-start | bytes 2097152 | tf_op jit(solution)/shard_map/psum | solution.py:254
  272.0 161.5 %all-gather.3.cloned.1.call-start = ((), (), s32[]{:S(2)}) async-start(), calls=%async_computation.9 | async-start | bytes 5570560 | tf_op jit(solution)/shard_map/all_gather | solution.py:255
  433.5 4.8 %copy-start.1 = (bf16[512,1024]{1,0:T(8,128)(2,1)S(1)}, bf16[512,1024]{1,0:T(8,128)(2,1)}, u32[]{:S(2)}) copy-start(bf16[512,1024]{1,0:T(8,128)(2,1)} %param.15) | copy-start | bytes 3145732
  (29 other events, 34.9 us)
Sparse Core Ops, SparseCore 0:
  182.7 101.0 reduce-scatter.1
Sparse Core Ops, SparseCore 1:
  272.1 98.7 all-reduce.1
  373.2 60.3 all-gather.2
